TPU v7x, 32 devices: a whole 2x2x4 slice. The times are simulated.
32 devices in a mesh: seq: 4 (over y, x), fsdp: 8 (over z, core).
Axes of the slice: x: 2, y: 2, z: 4, core: 2. Of those that a mesh axis runs over, the one named last changes fastest.
Arguments:
- tokens: bfloat16 [8, 1152, 2048], P('fsdp', 'seq'), may hold values from -6 to 6
- doc_lengths: int32 [8, 4], P('fsdp'), may hold values from 1 to 1024, as said below
- positions: int32 [8, 1152], P('fsdp'), may hold values from 0 to 2174, as said below
- cotangent: bfloat16 [8, 1152, 2048], P('fsdp', 'seq'), may hold values from -6 to 6
- w_query: bfloat16 [2048, 2048], P('fsdp'), may hold values from -0.125 to 0.125
- key_matrix: bfloat16 [2048, 1024], P('fsdp'), may hold values from -0.125 to 0.125
- value_matrix: bfloat16 [2048, 1024], P('fsdp'), may hold values from -0.125 to 0.125
- w_attn_gate: bfloat16 [2048, 2048], P('fsdp'), may hold values from -0.125 to 0.125
- w_out: bfloat16 [2048, 2048], P('fsdp'), may hold values from -1.5 to 1.5
- w_gate: bfloat16 [2048, 6144], P('fsdp'), may hold values from -0.125 to 0.125
- w_up: bfloat16 [2048, 6144], P('fsdp'), may hold values from -0.125 to 0.125
- w_down: bfloat16 [6144, 2048], P('fsdp'), may hold values from -0.078125 to 0.078125
- gain_attn: bfloat16 [2048], P('fsdp'), may hold values from 0.25 to 1.75
- gain_mlp: bfloat16 [2048], P('fsdp'), may hold values from 0.25 to 1.75
Outputs:
- block_output: bfloat16 [8, 1152, 2048], P('fsdp', 'seq')
- grad_tokens: bfloat16 [8, 1152, 2048], P('fsdp', 'seq')
- grad_w_query: float32 [2048, 2048], P('fsdp')
- grad_w_key: float32 [2048, 1024], P('fsdp')
- grad_w_value: float32 [2048, 1024], P('fsdp')
- grad_w_attn_gate: float32 [2048, 2048], P('fsdp')
- grad_w_out: float32 [2048, 2048], P('fsdp')
- grad_w_gate: float32 [2048, 6144], P('fsdp')
- grad_w_up: float32 [2048, 6144], P('fsdp')
- grad_w_down: float32 [6144, 2048], P('fsdp')
- grad_gain_attn: float32 [2048], P('fsdp')
- grad_gain_mlp: float32 [2048], P('fsdp')
Inputs may be any that keep to these rules, and one draw needn't show every extreme that they name: `doc_lengths`: each pack's 4 document lengths sum to 1152, and the largest is exactly 1024. `positions`: a token's position is its index within its document plus an offset shared by the whole document, below 1152; the longest document's offset is the largest.
All inputs are finite; a program needn't handle non-finite values.
Results may differ from a plain program's by a relative error of at most 0.02.
Values may be sent and summed in bfloat16 or wider, within the bound.
No kernel may reach another device: no remote copies, remote signals or barrier semaphores. Data moves between devices by JAX's collectives and lax.ppermute only.
A program may use at most 512 MiB of HBM per device.

v0:
```python
import jax
import jax.numpy as jnp
from jax import lax
from jax.sharding import PartitionSpec as P

QUERY_HEADS = 16
KEY_VALUE_HEADS = 8
HEAD_DIM = 128
QB = 576
epsilon = 1e-06
rope_base = 1000000.0
masked_value = -1e30


def dot_plain(left_mat, right_mat):
    return jnp.dot(left_mat, right_mat, preferred_element_type=jnp.float32)


def dot_rows(left_mat, right_mat):
    return lax.dot_general(
        left_mat, right_mat, (((0,), (0,)), ((), ())), preferred_element_type=jnp.float32
    )


def dot_back(left_mat, right_mat):
    return lax.dot_general(
        left_mat, right_mat, (((1,), (1,)), ((), ())), preferred_element_type=jnp.float32
    )


def rms_parts(values):
    inv_scale = lax.rsqrt(jnp.mean(values * values, axis=-1, keepdims=True) + epsilon)
    return (values * inv_scale, inv_scale)


def rms_back(grad_normed_out, normed, inv_scale, gain):
    grad_gain = jnp.sum(grad_normed_out * normed, axis=0)
    grad_normed = grad_normed_out * gain
    grad_input = inv_scale * (
        grad_normed - normed * jnp.mean(grad_normed * normed, axis=-1, keepdims=True)
    )
    return (grad_input, grad_gain)


def angles_of(positions):
    half_dim = HEAD_DIM // 2
    frequency = rope_base ** (-(2.0 * jnp.arange(half_dim, dtype=jnp.float32)) / HEAD_DIM)
    return positions.astype(jnp.float32)[:, None] * frequency[None, :]


def apply_rotation(values, rotary_angles):
    half_dim = values.shape[-1] // 2
    cosine = jnp.cos(rotary_angles)[:, None, :]
    sine_part = jnp.sin(rotary_angles)[:, None, :]
    leading = values[..., :half_dim]
    trailing = values[..., half_dim:]
    return jnp.concatenate(
        [leading * cosine - trailing * sine_part, trailing * cosine + leading * sine_part], axis=-1
    )


def shards(
    tokens,
    doc_lengths,
    positions,
    cotangent,
    w_query,
    key_matrix,
    value_matrix,
    w_attn_gate,
    w_out,
    w_gate,
    w_up,
    w_down,
    gain_attn,
    gain_mlp,
):
    inputs = tokens[0].astype(jnp.float32)
    local_rows = inputs.shape[0]
    grad_out = cotangent[0]
    normed_attn, scale_attn = rms_parts(inputs)
    full_query, full_key, full_value, full_attn_gate, full_out, full_gain_attn, full_gain_mlp = (
        lax.all_gather(w_query, "fsdp", axis=0, tiled=True),
        lax.all_gather(key_matrix, "fsdp", axis=0, tiled=True),
        lax.all_gather(value_matrix, "fsdp", axis=0, tiled=True),
        lax.all_gather(w_attn_gate, "fsdp", axis=0, tiled=True),
        lax.all_gather(w_out, "fsdp", axis=0, tiled=True),
        lax.all_gather(gain_attn, "fsdp", axis=0, tiled=True),
        lax.all_gather(gain_mlp, "fsdp", axis=0, tiled=True),
    )
    gain_attn_f = full_gain_attn.astype(jnp.float32)
    gain_mlp_f = full_gain_mlp.astype(jnp.float32)
    hidden_attention = (normed_attn * gain_attn_f).astype(jnp.bfloat16)
    query_rows = (
        dot_plain(hidden_attention, full_query)
        .astype(jnp.bfloat16)
        .reshape(local_rows, -1, HEAD_DIM)
    )
    keys_tok = (
        dot_plain(hidden_attention, full_key).astype(jnp.bfloat16).reshape(local_rows, -1, HEAD_DIM)
    )
    values_tok = (
        dot_plain(hidden_attention, full_value)
        .astype(jnp.bfloat16)
        .reshape(local_rows, -1, HEAD_DIM)
    )
    gates_tok = (
        dot_plain(hidden_attention, full_attn_gate)
        .astype(jnp.bfloat16)
        .reshape(local_rows, -1, HEAD_DIM)
    )
    q_heads, k_heads, v_heads, g_heads = (
        lax.all_to_all(query_rows, "seq", split_axis=1, concat_axis=0, tiled=True),
        lax.all_to_all(keys_tok, "seq", split_axis=1, concat_axis=0, tiled=True),
        lax.all_to_all(values_tok, "seq", split_axis=1, concat_axis=0, tiled=True),
        lax.all_to_all(gates_tok, "seq", split_axis=1, concat_axis=0, tiled=True),
    )
    pack_len = q_heads.shape[0]
    local_q = q_heads.shape[1]
    local_kv = k_heads.shape[1]
    query_group_width = QUERY_HEADS // KEY_VALUE_HEADS
    token_index = jnp.arange(pack_len, dtype=jnp.int32)
    doc_ends = jnp.cumsum(doc_lengths[0])
    segment = jnp.sum((token_index[:, None] >= doc_ends[None, :]).astype(jnp.int32), axis=1)
    rotary_angles = angles_of(positions[0])
    q_rot = (
        apply_rotation(q_heads.astype(jnp.float32), rotary_angles)
        .astype(jnp.bfloat16)
        .reshape(pack_len, local_kv, query_group_width, HEAD_DIM)
    )
    k_rot = apply_rotation(k_heads.astype(jnp.float32), rotary_angles).astype(jnp.bfloat16)
    scale_factor = HEAD_DIM ** (-0.5)
    block_starts = jnp.arange(pack_len // QB, dtype=jnp.int32) * QB

    def block_scores(block_start):
        q_block = lax.dynamic_slice_in_dim(q_rot, block_start, QB, 0)
        raw_scores = (
            jnp.einsum("qhgd,khd->hgqk", q_block, k_rot, preferred_element_type=jnp.float32)
            * scale_factor
        )
        row_ids = block_start + jnp.arange(QB, dtype=jnp.int32)
        row_segment = lax.dynamic_slice_in_dim(segment, block_start, QB, 0)
        allowed = (row_segment[:, None] == segment[None, :]) & (
            row_ids[:, None] >= token_index[None, :]
        )
        return (q_block, jnp.where(allowed[None, None], raw_scores, masked_value))

    def attend_block(block_start):
        q_block, scores = block_scores(block_start)
        row_max = jnp.max(scores, axis=-1, keepdims=True)
        exp_scores = jnp.exp(scores - row_max)
        row_total = jnp.sum(exp_scores, axis=-1, keepdims=True)
        attn_probs = exp_scores / row_total
        log_total = (row_max + jnp.log(row_total))[..., 0]
        mixed_block = jnp.einsum(
            "hgqk,khd->qhgd",
            attn_probs.astype(jnp.bfloat16),
            v_heads,
            preferred_element_type=jnp.float32,
        )
        return (mixed_block, log_total)

    mixed_blocks, lse_blocks = lax.map(attend_block, block_starts)
    mixed_heads = mixed_blocks.reshape(pack_len, local_q, HEAD_DIM)
    gate_sig = jax.nn.sigmoid(g_heads.astype(jnp.float32))
    gated_heads = (mixed_heads * gate_sig).astype(jnp.bfloat16)
    gated_tok = lax.all_to_all(gated_heads, "seq", split_axis=0, concat_axis=1, tiled=True).reshape(
        local_rows, -1
    )
    residual = inputs + dot_plain(gated_tok, full_out)
    normed_mlp, scale_mlp = rms_parts(residual)
    h_mlp = (normed_mlp * gain_mlp_f).astype(jnp.bfloat16)
    full_gate, full_up, full_down = (
        lax.all_gather(w_gate, "fsdp", axis=0, tiled=True),
        lax.all_gather(w_up, "fsdp", axis=0, tiled=True),
        lax.all_gather(w_down, "fsdp", axis=0, tiled=True),
    )
    gate_pre = dot_plain(h_mlp, full_gate)
    up_pre = dot_plain(h_mlp, full_up)
    sig_gate = jax.nn.sigmoid(gate_pre)
    silu_gate = gate_pre * sig_gate
    hidden = (silu_gate * up_pre).astype(jnp.bfloat16)
    output = residual + dot_plain(hidden, full_down)
    grad_hidden = dot_back(grad_out, full_down)
    grad_gate_pre = (grad_hidden * up_pre * sig_gate * (1.0 + gate_pre * (1.0 - sig_gate))).astype(
        jnp.bfloat16
    )
    grad_up_pre = (grad_hidden * silu_gate).astype(jnp.bfloat16)
    grad_gate_up = jnp.concatenate([grad_gate_pre, grad_up_pre], axis=1)
    gate_up_part = lax.psum_scatter(
        dot_rows(h_mlp, grad_gate_up).astype(jnp.bfloat16), "fsdp", scatter_dimension=0, tiled=True
    )
    down_part = lax.psum_scatter(
        dot_rows(hidden, grad_out).astype(jnp.bfloat16), "fsdp", scatter_dimension=0, tiled=True
    )
    grad_h_mlp = dot_back(grad_gate_pre, full_gate) + dot_back(grad_up_pre, full_up)
    grad_res_mlp, grad_gain_mlp = rms_back(grad_h_mlp, normed_mlp, scale_mlp, gain_mlp_f)
    grad_resid = grad_out.astype(jnp.float32) + grad_res_mlp
    grad_attn_out = grad_resid.astype(jnp.bfloat16)
    grad_w_out = dot_rows(gated_tok, grad_attn_out)
    grad_gated = (
        dot_back(grad_attn_out, full_out).astype(jnp.bfloat16).reshape(local_rows, -1, HEAD_DIM)
    )
    grad_gated_heads = lax.all_to_all(
        grad_gated, "seq", split_axis=1, concat_axis=0, tiled=True
    ).astype(jnp.float32)
    grad_mixed = (
        (grad_gated_heads * gate_sig)
        .astype(jnp.bfloat16)
        .reshape(pack_len, local_kv, query_group_width, HEAD_DIM)
    )
    grad_gate_logits = (grad_gated_heads * mixed_heads * gate_sig * (1.0 - gate_sig)).astype(
        jnp.bfloat16
    )

    def back_block(state_in, block_items):
        grad_keys, grad_values = state_in
        block_start, log_total = block_items
        q_block, scores = block_scores(block_start)
        attn_probs = jnp.exp(scores - log_total[..., None])
        grad_block = lax.dynamic_slice_in_dim(grad_mixed, block_start, QB, 0)
        grad_probs = jnp.einsum(
            "qhgd,khd->hgqk", grad_block, v_heads, preferred_element_type=jnp.float32
        )
        row_delta = jnp.sum(attn_probs * grad_probs, axis=-1, keepdims=True)
        grad_scores = (attn_probs * (grad_probs - row_delta) * scale_factor).astype(jnp.bfloat16)
        grad_q_block = jnp.einsum(
            "hgqk,khd->qhgd", grad_scores, k_rot, preferred_element_type=jnp.float32
        )
        grad_keys = grad_keys + jnp.einsum(
            "hgqk,qhgd->khd", grad_scores, q_block, preferred_element_type=jnp.float32
        )
        grad_values = grad_values + jnp.einsum(
            "hgqk,qhgd->khd",
            attn_probs.astype(jnp.bfloat16),
            grad_block,
            preferred_element_type=jnp.float32,
        )
        return ((grad_keys, grad_values), grad_q_block)

    zero_keys = jnp.zeros((pack_len, local_kv, HEAD_DIM), jnp.float32)
    (grad_k_sum, grad_v_sum), grad_q_blocks = lax.scan(
        back_block, (zero_keys, zero_keys), (block_starts, lse_blocks)
    )
    grad_q = apply_rotation(
        grad_q_blocks.reshape(pack_len, local_q, HEAD_DIM), -rotary_angles
    ).astype(jnp.bfloat16)
    grad_k = apply_rotation(grad_k_sum, -rotary_angles).astype(jnp.bfloat16)
    grad_v = grad_v_sum.astype(jnp.bfloat16)
    dq_tok, dk_tok, dv_tok, dg_tok = (
        lax.all_to_all(grad_q, "seq", split_axis=0, concat_axis=1, tiled=True),
        lax.all_to_all(grad_k, "seq", split_axis=0, concat_axis=1, tiled=True),
        lax.all_to_all(grad_v, "seq", split_axis=0, concat_axis=1, tiled=True),
        lax.all_to_all(grad_gate_logits, "seq", split_axis=0, concat_axis=1, tiled=True),
    )
    dq_tok = dq_tok.reshape(local_rows, -1)
    dk_tok = dk_tok.reshape(local_rows, -1)
    dv_tok = dv_tok.reshape(local_rows, -1)
    dg_tok = dg_tok.reshape(local_rows, -1)
    grad_w_query = dot_rows(hidden_attention, dq_tok)
    grad_w_key = dot_rows(hidden_attention, dk_tok)
    grad_w_value = dot_rows(hidden_attention, dv_tok)
    grad_w_attn_gate = dot_rows(hidden_attention, dg_tok)
    grad_h_attn = (
        dot_back(dq_tok, full_query)
        + dot_back(dk_tok, full_key)
        + dot_back(dv_tok, full_value)
        + dot_back(dg_tok, full_attn_gate)
    )
    grad_res_attn, grad_gain_attn = rms_back(grad_h_attn, normed_attn, scale_attn, gain_attn_f)
    grad_tokens = (grad_resid + grad_res_attn).astype(jnp.bfloat16)[None]
    part_query, part_key, part_value, part_attn_gate, part_out, part_gain_attn, part_gain_mlp = (
        lax.psum_scatter(
            grad_w_query.astype(jnp.bfloat16), "fsdp", scatter_dimension=0, tiled=True
        ).astype(jnp.float32),
        lax.psum_scatter(
            grad_w_key.astype(jnp.bfloat16), "fsdp", scatter_dimension=0, tiled=True
        ).astype(jnp.float32),
        lax.psum_scatter(
            grad_w_value.astype(jnp.bfloat16), "fsdp", scatter_dimension=0, tiled=True
        ).astype(jnp.float32),
        lax.psum_scatter(
            grad_w_attn_gate.astype(jnp.bfloat16), "fsdp", scatter_dimension=0, tiled=True
        ).astype(jnp.float32),
        lax.psum_scatter(
            grad_w_out.astype(jnp.bfloat16), "fsdp", scatter_dimension=0, tiled=True
        ).astype(jnp.float32),
        lax.psum_scatter(
            grad_gain_attn.astype(jnp.bfloat16), "fsdp", scatter_dimension=0, tiled=True
        ).astype(jnp.float32),
        lax.psum_scatter(
            grad_gain_mlp.astype(jnp.bfloat16), "fsdp", scatter_dimension=0, tiled=True
        ).astype(jnp.float32),
    )
    (
        sum_gate_up,
        sum_down,
        sum_query,
        sum_key,
        sum_value,
        sum_attn_gate,
        sum_out,
        sum_gain_attn,
        sum_gain_mlp,
    ) = (
        lax.psum(gate_up_part, "seq").astype(jnp.float32),
        lax.psum(down_part, "seq").astype(jnp.float32),
        lax.psum(part_query.astype(jnp.bfloat16), "seq").astype(jnp.float32),
        lax.psum(part_key.astype(jnp.bfloat16), "seq").astype(jnp.float32),
        lax.psum(part_value.astype(jnp.bfloat16), "seq").astype(jnp.float32),
        lax.psum(part_attn_gate.astype(jnp.bfloat16), "seq").astype(jnp.float32),
        lax.psum(part_out.astype(jnp.bfloat16), "seq").astype(jnp.float32),
        lax.psum(part_gain_attn.astype(jnp.bfloat16), "seq").astype(jnp.float32),
        lax.psum(part_gain_mlp.astype(jnp.bfloat16), "seq").astype(jnp.float32),
    )
    split_at = sum_gate_up.shape[1] // 2
    sum_gate = sum_gate_up[:, :split_at]
    sum_up = sum_gate_up[:, split_at:]
    return (
        output.astype(jnp.bfloat16)[None],
        grad_tokens,
        sum_query,
        sum_key,
        sum_value,
        sum_attn_gate,
        sum_out,
        sum_gate,
        sum_up,
        sum_down,
        sum_gain_attn,
        sum_gain_mlp,
    )


def solution(mesh):
    in_specs = (
        P("fsdp", "seq", None),
        P("fsdp", None),
        P("fsdp", None),
        P("fsdp", "seq", None),
        P("fsdp", None),
        P("fsdp", None),
        P("fsdp", None),
        P("fsdp", None),
        P("fsdp", None),
        P("fsdp", None),
        P("fsdp", None),
        P("fsdp", None),
        P("fsdp"),
        P("fsdp"),
    )
    out_specs = (
        P("fsdp", "seq", None),
        P("fsdp", "seq", None),
        P("fsdp", None),
        P("fsdp", None),
        P("fsdp", None),
        P("fsdp", None),
        P("fsdp", None),
        P("fsdp", None),
        P("fsdp", None),
        P("fsdp", None),
        P("fsdp"),
        P("fsdp"),
    )
    return jax.shard_map(shards, mesh=mesh, in_specs=in_specs, out_specs=out_specs, check_vma=False)
```

profile of v0, /device:TPU:0, one launch (start us, length us, event | category | flops | bytes accessed | tf_op | source)
XLA Modules:
  0.0 2623.2 jit_solution(13021053463534006150)
XLA Ops:
  33.1 26.1 all-gather.13.cloned.1.call-done
  67.4 39.1 %all-gather.15.cloned.1.call-done = bf16[2048,1024]{1,0:T(8,128)(2,1)} async-done(((bf16[256,1024]{1,0:T(8,128)(2,1)}), bf16[2048,1024]{1,0:T(8,128)(2,1)}) %all-gather.15.cloned.1.call-update) | async-done | bytes 4194320 | tf_op jit(solution)/shard_map/all_gather | solution.py:85
  114.7 74.3 %all-gather.11.cloned.1.call-done = bf16[2048,2048]{1,0:T(8,128)(2,1)} async-done(((bf16[256,2048]{1,0:T(8,128)(2,1)}), bf16[2048,2048]{1,0:T(8,128)(2,1)}) %all-gather.11.cloned.1.call-update) | async-done | bytes 8388624 | tf_op jit(solution)/shard_map/all_gather | solution.py:83
  201.8 69.2 %all-gather.17.cloned.1.call-done = bf16[2048,2048]{1,0:T(8,128)(2,1)} async-done(((bf16[256,2048]{1,0:T(8,128)(2,1)}), bf16[2048,2048]{1,0:T(8,128)(2,1)}) %all-gather.17.cloned.1.call-update) | async-done | bytes 8388624 | tf_op jit(solution)/shard_map/all_gather | solution.py:86
  306.2 32.7 %while.28 = (s32[]{:T(128)}, f32[2,576,2,2,128]{4,1,0,3,2:T(8,128)}, f32[2,2,2,576]{3,2,1,0:T(2,128)}, s32[2]{0:T(128)S(1)}, s32[1152]{0:T(1024)S(1)}, /*index=5...) while((s32[]{:T(128)}, ...), condition=%wide.region_6.7_spmd.clone, body=%wide.region_3.6_spmd.clone.sunk | while | flops 1392793856 | bytes 37545896 | solution.py:163
  375.1 197.8 %all-gather.21.cloned.1.call-done = bf16[2048,6144]{1,0:T(8,128)(2,1)} async-done(((bf16[256,6144]{1,0:T(8,128)(2,1)}), bf16[2048,6144]{1,0:T(8,128)(2,1)}) %all-gather.21.cloned.1.call-update) | async-done | bytes 25165840 | tf_op jit(solution)/shard_map/all_gather | solution.py:174
  572.9 16.4 fusion.106
  589.2 203.3 %all-gather.23.cloned.1.call-done = bf16[2048,6144]{1,0:T(8,128)(2,1)} async-done(((bf16[256,6144]{1,0:T(8,128)(2,1)}), bf16[2048,6144]{1,0:T(8,128)(2,1)}) %all-gather.23.cloned.1.call-update) | async-done | bytes 25165840 | tf_op jit(solution)/shard_map/all_gather | solution.py:175
  807.8 204.5 %all-gather.25.cloned.1.call-done = bf16[6144,2048]{1,0:T(8,128)(2,1)} async-done(((bf16[768,2048]{1,0:T(8,128)(2,1)}), bf16[6144,2048]{1,0:T(8,128)(2,1)}) %all-gather.25.cloned.1.call-update) | async-done | bytes 25165840 | tf_op jit(solution)/shard_map/all_gather | solution.py:176
  1012.3 20.9 multiply_convert_fusion
  1047.7 15.7 multiply_reduce_fusion
  1097.9 114.7 %while.29 = (s32[]{:T(128)}, f32[1152,2,128]{0,2,1:T(8,128)}, f32[1152,2,128]{0,2,1:T(8,128)S(1)}, f32[2,576,2,2,128]{4,1,0,3,2:T(8,128)}, s32[2]{0:T(128)S(1)},...) while((s32[]{:T(128)}, f32[1152,2,128]{0,2,1:T(8,128)}, ...), condition=%wide.region_11.12_spmd.clone, body=%wide.region_9.11_spmd.clone.sunk | while | flops 3437723136 | bytes 128183776 | solution.py:242
  1116.2 16.4 fusion.182
  1132.6 17.1 fusion.180
  1173.3 16.4 fusion.182
  1189.7 17.4 fusion.180
  1332.2 18.7 convolution_convert_fusion.1
  1352.2 33.7 %convolution_convert_fusion = bf16[2048,12288]{1,0:T(8,128)(2,1)} fusion(bf16[288,2048]{1,0:T(8,128)(2,1)S(1)} %copy-done.27, bf16[288,6144]{1,0:T(8,128)(2,1)} %get-tuple-element.240, bf16[288,6144]{1,0:T(8,128)(2,1)} %get-tuple-element.241), kind=kOutput, calls=%fused_computation.61 | convolution fusion | flops 14534836224 | bytes 58589184 | tf_op jit(solution)/shard_map/dot_general | solution.py:20
  1386.0 38.3 %reduce-scatter.18.cloned.1.call-done = bf16[256,2048]{1,0:T(8,128)(2,1)} async-done(((bf16[2048,2048]{1,0:T(8,128)(2,1)}), bf16[256,2048]{1,0:T(8,128)(2,1)}) %reduce-scatter.18.cloned.1.call-update) | async-done | bytes 1048592 | tf_op jit(solution)/shard_map/reduce_scatter | solution.py:285
  1424.4 90.2 %reduce-scatter.10.cloned.1.call-done = bf16[256,2048]{1,0:T(8,128)(2,1)} async-done(((bf16[2048,2048]{1,0:T(8,128)(2,1)}), bf16[256,2048]{1,0:T(8,128)(2,1)}) %reduce-scatter.10.cloned.1.call-update) | async-done | bytes 1048592 | tf_op jit(solution)/shard_map/reduce_scatter | solution.py:273
  1514.5 90.3 %reduce-scatter.16.cloned.1.call-done = bf16[256,2048]{1,0:T(8,128)(2,1)} async-done(((bf16[2048,2048]{1,0:T(8,128)(2,1)}), bf16[256,2048]{1,0:T(8,128)(2,1)}) %reduce-scatter.16.cloned.1.call-update) | async-done | bytes 1048592 | tf_op jit(solution)/shard_map/reduce_scatter | solution.py:282
  1604.8 247.8 %reduce-scatter.20.cloned.1.call-done = bf16[768,2048]{1,0:T(8,128)(2,1)} async-done(((bf16[6144,2048]{1,0:T(8,128)(2,1)}), bf16[768,2048]{1,0:T(8,128)(2,1)}) %reduce-scatter.20.cloned.1.call-update) | async-done | bytes 3145744 | tf_op jit(solution)/shard_map/reduce_scatter | solution.py:193
  1852.6 483.8 %reduce-scatter.22.cloned.1.call-done = bf16[256,12288]{1,0:T(8,128)(2,1)} async-done(((bf16[2048,12288]{1,0:T(8,128)(2,1)}), bf16[256,12288]{1,0:T(8,128)(2,1)}) %reduce-scatter.22.cloned.1.call-update) | async-done | bytes 6291472
  2402.8 193.6 %all-reduce.8.cloned.1.call-done = (bf16[256,2048]{1,0:T(8,128)(2,1)}, bf16[256,1024]{1,0:T(8,128)(2,1)}, bf16[256,1024]{1,0:T(8,128)(2,1)}, bf16[256,2048]{1,0:...) async-done(((bf16[256,2048]{1,0:T(8,128)(2,1)}, bf16[256,1024]{1,0:T(8,128)(2,1)}, bf16[256,1024]{1,0:T(8,128)(2,1)}, ...) | async-done | bytes 13631504 | tf_op jit(solution)/shard_map/psum | solution.py:308
  (289 shorter events, 468.1 us)
Async XLA Ops:
  7.2 52.0 %all-gather.13.cloned.1.call-start = ((), (), s32[]{:S(2)}) async-start(), calls=%async_computation.18 | async-start | bytes 4718592 | tf_op jit(solution)/shard_map/all_gather | solution.py:84
  7.9 98.6 %all-gather.15.cloned.1.call-start = ((), (), s32[]{:S(2)}) async-start(), calls=%async_computation.19 | async-start | bytes 4718592 | tf_op jit(solution)/shard_map/all_gather | solution.py:85
  8.7 180.3 %all-gather.11.cloned.1.call-start = ((), (), s32[]{:S(2)}) async-start(), calls=%async_computation.17 | async-start | bytes 9437184 | tf_op jit(solution)/shard_map/all_gather | solution.py:83
  9.4 261.6 %all-gather.17.cloned.1.call-start = ((), (), s32[]{:S(2)}) async-start(), calls=%async_computation.20 | async-start | bytes 9437184 | tf_op jit(solution)/shard_map/all_gather | solution.py:86
  10.0 358.3 %all-gather.19.cloned.1.call-start = ((), (), s32[]{:S(2)}) async-start(), calls=%async_computation.21 | async-start | bytes 9437184 | tf_op jit(solution)/shard_map/all_gather | solution.py:87
  10.6 562.3 %all-gather.21.cloned.1.call-start = ((), (), s32[]{:S(2)}) async-start(), calls=%async_computation.22 | async-start | bytes 28311552 | tf_op jit(solution)/shard_map/all_gather | solution.py:174
  11.1 781.4 %all-gather.23.cloned.1.call-start = ((), (), s32[]{:S(2)}) async-start(), calls=%async_computation.23 | async-start | bytes 28311552 | tf_op jit(solution)/shard_map/all_gather | solution.py:175
  11.9 1000.4 %all-gather.25.cloned.1.call-start = ((), (), s32[]{:S(2)}) async-start(), calls=%async_computation.24 | async-start | bytes 28311552 | tf_op jit(solution)/shard_map/all_gather | solution.py:176
  63.8 47.3 %all-to-all-start.1 = ((bf16[288,8,128]{2,0,1:T(8,128)(2,1)}), bf16[288,8,128]{2,0,1:T(8,128)(2,1)S(1)}, u32[]{:S(2)}, u32[]{:S(2)}) async-start(bf16[288,8,128]{2,0,1:T(8,128)(2,1)} %bitcast.295), calls=%async_computation.1 | async-start | bytes 1179648 | tf_op jit(solution)/shard_map/all_to_all | solution.py:114
  111.1 85.2 %all-to-all-start.2 = ((bf16[288,8,128]{2,0,1:T(8,128)(2,1)}), bf16[288,8,128]{2,0,1:T(8,128)(2,1)S(1)}, u32[]{:S(2)}, u32[]{:S(2)}) async-start(bf16[288,8,128]{2,0,1:T(8,128)(2,1)} %bitcast.294), calls=%async_computation.2 | async-start | bytes 1179648 | tf_op jit(solution)/shard_map/all_to_all | solution.py:115
  196.3 82.0 %all-to-all-start = ((bf16[288,16,128]{2,0,1:T(8,128)(2,1)}), bf16[288,16,128]{2,0,1:T(8,128)(2,1)}, u32[]{:S(2)}, u32[]{:S(2)}) async-start(bf16[288,16,128]{2,0,1:T(8,128)(2,1)} %bitcast.290), calls=%async_computation | async-start | bytes 2359296 | tf_op jit(solution)/shard_map/all_to_all | solution.py:113
  278.3 20.3 all-to-all-start.3
  347.8 18.4 all-to-all-start.4
  374.2 689.9 %copy-start.10 = (f32[288,2048]{1,0:T(8,128)}, f32[288,2048]{1,0:T(8,128)S(1)}, u32[]{:S(2)}) copy-start(f32[288,2048]{1,0:T(8,128)S(1)} %get-tuple-element.258) | copy-start | bytes 7077892
  589.2 423.0 %copy-start.24 = (bf16[1,288,2048]{2,1,0:T(8,128)(2,1)S(1)}, bf16[1,288,2048]{2,1,0:T(8,128)(2,1)}, u32[]{:S(2)}) copy-start(bf16[1,288,2048]{2,1,0:T(8,128)(2,1)} %param.21) | copy-start | bytes 3538948
  1074.6 19.2 all-to-all-start.5
  1078.2 307.8 %reduce-scatter.12.cloned.1.call-start = ((), (), s32[]{:S(2)}) async-start(), calls=%async_computation.26 | async-start | bytes 4718592 | tf_op jit(solution)/shard_map/reduce_scatter | solution.py:276
  1236.3 149.8 %reduce-scatter.14.cloned.1.call-start = ((), (), s32[]{:S(2)}) async-start(), calls=%async_computation.27 | async-start | bytes 4718592 | tf_op jit(solution)/shard_map/reduce_scatter | solution.py:279
  1253.7 170.6 %reduce-scatter.18.cloned.1.call-start = ((), (), s32[]{:S(2)}) async-start(), calls=%async_computation.29 | async-start | bytes 9437184 | tf_op jit(solution)/shard_map/reduce_scatter | solution.py:285
  1263.6 251.0 %reduce-scatter.10.cloned.1.call-start = ((), (), s32[]{:S(2)}) async-start(), calls=%async_computation.25 | async-start | bytes 9437184 | tf_op jit(solution)/shard_map/reduce_scatter | solution.py:273
  1297.5 307.4 %reduce-scatter.16.cloned.1.call-start = ((), (), s32[]{:S(2)}) async-start(), calls=%async_computation.28 | async-start | bytes 9437184 | tf_op jit(solution)/shard_map/reduce_scatter | solution.py:282
  1331.0 521.7 %reduce-scatter.20.cloned.1.call-start = ((), (), s32[]{:S(2)}) async-start(), calls=%async_computation.30 | async-start | bytes 28311552 | tf_op jit(solution)/shard_map/reduce_scatter | solution.py:193
  1350.9 985.5 %reduce-scatter.22.cloned.1.call-start = ((), (), s32[]{:S(2)}) async-start(), calls=%async_computation.31 | async-start | bytes 56623104
  1385.9 1210.4 %all-reduce.8.cloned.1.call-start = ((), (), s32[]{:S(2)}) async-start(), calls=%async_computation.32 | async-start | bytes 27262976 | tf_op jit(solution)/shard_map/psum | solution.py:308
  (51 other events, 860.6 us)
Sparse Core Ops, SparseCore 0:
  9.6 49.5 all-gather.12
  60.8 45.6 all-gather.14
  108.1 80.8 all-gather.10
  190.5 80.5 all-gather.16
  272.5 80.5 all-gather.18
  354.5 218.3 all-gather.20
  574.5 218.0 all-gather.22
  794.2 218.0 all-gather.24
  1236.4 46.4 reduce-scatter.11
  1285.6 48.3 reduce-scatter.13
  1336.3 87.9 reduce-scatter.17
  1426.5 87.9 reduce-scatter.9
  1516.8 87.9 reduce-scatter.15
  1607.1 245.5 reduce-scatter.19
  1854.9 481.4 reduce-scatter.21
  2341.0 255.2 all-reduce.7
where the time goes:
time: 2630 us; the launch traced here: 2620 us
  waiting for transfers between devices  2000 us (76%)
  matrix products  350 us (13%)
  blocking collectives  99.9 us (4%)
  local copies, waits for them, and re-layouts  66.6 us (3%)
  other arithmetic  60.9 us (2%)
    unnamed x17, waiting for transfers between devices  489 us
    reduce_scatter x1, waiting for transfers between devices, shards(): lax.psum_scatter(dot_rows(hidden, grad_out).astype(jnp.bfloat16), 'fsdp',...  248 us
    all_gather x1, waiting for transfers between devices, shards(): lax.all_gather(w_down, 'fsdp', axis=0, tiled=True)  204 us
    all_gather x1, waiting for transfers between devices, shards(): lax.all_gather(w_up, 'fsdp', axis=0, tiled=True)  203 us
    all_gather x1, waiting for transfers between devices, shards(): lax.all_gather(w_gate, 'fsdp', axis=0, tiled=True)  198 us
    psum x1, waiting for transfers between devices, shards(): lax.psum(part_query.astype(jnp.bfloat16), 'seq').astype(jnp.float32)  194 us
    reduce_scatter x1, waiting for transfers between devices, shards(): lax.psum_scatter(grad_w_attn_gate.astype(jnp.bfloat16), 'fsdp', scatter_d...  90.3 us
    reduce_scatter x1, waiting for transfers between devices, shards(): lax.psum_scatter(grad_w_query.astype(jnp.bfloat16), 'fsdp', scatter_dimen...  90.2 us
  transfers between devices with their start and end apart: 22, of which 16 were waited for; matrix products, arithmetic and copies ran while one was open for 10% of the time, Pallas kernels for 0%

commit v1 on v0

--- a/solution.py
+++ b/solution.py
@@ -1,3 +1,4 @@
+import functools
 import jax
 import jax.numpy as jnp
 from jax import lax
@@ -10,6 +11,33 @@
 epsilon = 1e-06
 rope_base = 1000000.0
 masked_value = -1e30
+
+
+def lead_bands_by_axis(inner_x, at_axis):
+    row_out, v_now, response = (
+        lax.axis_size("fsdp"),
+        lax.axis_index("fsdp"),
+        inner_x.shape[at_axis],
+    )
+    block_last, odd = (inner_x, 1)
+    while odd < row_out:
+        block_last = jnp.concatenate(
+            [
+                block_last,
+                lax.ppermute(
+                    block_last,
+                    "fsdp",
+                    perm=tuple(((j, (j - odd) % row_out) for j in range(row_out))),
+                ),
+            ],
+            axis=at_axis,
+        )
+        odd = 2 * odd
+    s_next = jnp.roll(block_last, shift=v_now * response, axis=at_axis)
+    return s_next
+
+
+launch_meshes_in = functools.partial(lead_bands_by_axis, at_axis=0)
 
 
 def dot_plain(left_mat, right_mat):
@@ -83,7 +111,7 @@
         lax.all_gather(w_query, "fsdp", axis=0, tiled=True),
         lax.all_gather(key_matrix, "fsdp", axis=0, tiled=True),
         lax.all_gather(value_matrix, "fsdp", axis=0, tiled=True),
-        lax.all_gather(w_attn_gate, "fsdp", axis=0, tiled=True),
+        launch_meshes_in(w_attn_gate),
         lax.all_gather(w_out, "fsdp", axis=0, tiled=True),
         lax.all_gather(gain_attn, "fsdp", axis=0, tiled=True),
         lax.all_gather(gain_mlp, "fsdp", axis=0, tiled=True),

time: 2630 us -> 2750 us (1.046)
  blocking collectives: 99.9 us -> 237 us
  waiting for transfers between devices: 2000 us -> 1940 us
    ppermute x0 -> x3, waiting for transfers between devices: none -> 267 us  [lead_bands_by_axis(): lax.ppermute(block_last, 'fsdp', perm=tuple(((j, (j - odd) % row_out) for...]
    all_gather x1, waiting for transfers between devices: 198 us -> 88.6 us  [shards(): lax.all_gather(w_gate, 'fsdp', axis=0, tiled=True)]
    all_gather x1, blocking collectives: 13.6 us -> 115 us  [shards(): lax.all_gather(gain_attn, 'fsdp', axis=0, tiled=True)]
    all_gather x1, waiting for transfers between devices: 74.3 us -> 0.02 us  [shards(): lax.all_gather(w_query, 'fsdp', axis=0, tiled=True)]
    all_gather x1 -> x0, waiting for transfers between devices: 69.2 us -> none  [shards(): lax.all_gather(w_attn_gate, 'fsdp', axis=0, tiled=True)]
    all_gather x1, waiting for transfers between devices: 39.1 us -> 0.01 us  [shards(): lax.all_gather(value_matrix, 'fsdp', axis=0, tiled=True)]
    all_gather x1, blocking collectives: 8.98 us -> 42.4 us  [shards(): lax.all_gather(gain_mlp, 'fsdp', axis=0, tiled=True)]
    unnamed x17 -> x16, waiting for transfers between devices: 489 us -> 488 us
  transfers between devices with their start and end apart: 22 -> 24, of which waited for: 16 -> 16; matrix products, arithmetic and copies ran while one was open for 10% -> 10% of each run, Pallas kernels for 0% -> 0%
where the time goes in v1:
time: 2750 us; the launch traced here: 2740 us
  waiting for transfers between devices  1940 us (71%)
  matrix products  356 us (13%)
  blocking collectives  237 us (9%)
  local copies, waits for them, and re-layouts  90 us (3%)
  other arithmetic  61 us (2%)
  starting transfers between devices  31.5 us (1%)
    unnamed x16, waiting for transfers between devices  488 us
    ppermute x3, waiting for transfers between devices, lead_bands_by_axis(): lax.ppermute(block_last, 'fsdp', perm=tuple(((j, (j - odd) % row_out) for...  267 us
    reduce_scatter x1, waiting for transfers between devices, shards(): lax.psum_scatter(dot_rows(hidden, grad_out).astype(jnp.bfloat16), 'fsdp',...  248 us
    all_gather x1, waiting for transfers between devices, shards(): lax.all_gather(w_down, 'fsdp', axis=0, tiled=True)  204 us
    all_gather x1, waiting for transfers between devices, shards(): lax.all_gather(w_up, 'fsdp', axis=0, tiled=True)  203 us
    psum x1, waiting for transfers between devices, shards(): lax.psum(part_query.astype(jnp.bfloat16), 'seq').astype(jnp.float32)  190 us
    all_gather x1, blocking collectives, shards(): lax.all_gather(gain_attn, 'fsdp', axis=0, tiled=True)  115 us
    reduce_scatter x1, waiting for transfers between devices, shards(): lax.psum_scatter(grad_w_attn_gate.astype(jnp.bfloat16), 'fsdp', scatter_d...  90.3 us
  transfers between devices with their start and end apart: 24, of which 16 were waited for; matrix products, arithmetic and copies ran while one was open for 10% of the time, Pallas kernels for 0%

profile of v1, /device:TPU:0, one launch (start us, length us, event | category | flops | bytes accessed | tf_op | source)
XLA Modules:
  0.0 2739.5 jit_solution(18174893354743430318)
XLA Ops:
  16.5 28.7 %collective-permute-done = bf16[256,2048]{1,0:T(8,128)(2,1)S(1)} collective-permute-done((bf16[256,2048]{1,0:T(8,128)(2,1)S(1)}, bf16[256,2048]{1,0:T(8,128)(2,1)S(1)}, u32[]{:S(2)}, u32[]{:S(2)}) %collective-permute-start) | collective-permute-done | bytes 1048608 | tf_op jit(solution)/shard_map/ppermute | solution.py:27
  45.5 60.9 %collective-permute-done.1 = bf16[512,2048]{1,0:T(8,128)(2,1)S(1)} collective-permute-done((bf16[512,2048]{1,0:T(8,128)(2,1)S(1)}, bf16[512,2048]{1,0:T(8,128)(2,1)S(1)}, u32[]{:S(2)}, u32[]{:S(2)}) %collective-permute-start.1) | collective-permute-done | bytes 2097184 | tf_op jit(solution)/shard_map/ppermute | solution.py:27
  111.2 115.3 %all-gather = bf16[8,1,256]{2,1,0:T(2,128)(2,1)S(1)} all-gather(bf16[1,1,256]{2,1,0:T(2,128)(2,1)S(1)} %reshape.498), channel_id=1, replica_groups=mesh['seq'=4,'fsdp'=8] {'fsdp'}, dimensions={0}, use_global_device_ids=true | all-gather | bytes 4608 | tf_op jit(solution)/shard_map/all_gather | solution.py:116
  246.8 177.1 %collective-permute-done.2 = bf16[1024,2048]{1,0:T(8,128)(2,1)} collective-permute-done((bf16[1024,2048]{1,0:T(8,128)(2,1)}, bf16[1024,2048]{1,0:T(8,128)(2,1)}, u32[]{:S(2)}, u32[]{:S(2)}) %collective-permute-start.2) | collective-permute-done | bytes 4194336 | tf_op jit(solution)/shard_map/ppermute | solution.py:27
  501.3 32.6 %while.28 = (s32[]{:T(128)}, f32[2,576,2,2,128]{4,1,0,3,2:T(8,128)}, f32[2,2,2,576]{3,2,1,0:T(2,128)}, s32[2]{0:T(128)S(1)}, s32[1152]{0:T(1024)S(1)}, /*index=5...) while((s32[]{:T(128)}, ...), condition=%wide.region_6.7_spmd.clone, body=%wide.region_3.6_spmd.clone.sunk | while | flops 1392793856 | bytes 37545896 | solution.py:191
  546.4 42.4 %all-gather.1 = bf16[8,1,256]{2,1,0:T(2,128)(2,1)S(1)} all-gather(bf16[1,1,256]{2,1,0:T(2,128)(2,1)S(1)} %reshape.500), channel_id=1, replica_groups=mesh['seq'=4,'fsdp'=8] {'fsdp'}, dimensions={0}, use_global_device_ids=true | all-gather | bytes 4608 | tf_op jit(solution)/shard_map/all_gather | solution.py:117
  597.5 88.6 %all-gather.18.cloned.1.call-done = bf16[2048,6144]{1,0:T(8,128)(2,1)} async-done(((bf16[256,6144]{1,0:T(8,128)(2,1)}), bf16[2048,6144]{1,0:T(8,128)(2,1)}) %all-gather.18.cloned.1.call-update) | async-done | bytes 25165840 | tf_op jit(solution)/shard_map/all_gather | solution.py:202
  686.1 16.2 fusion.119
  702.3 203.3 %all-gather.20.cloned.1.call-done = bf16[2048,6144]{1,0:T(8,128)(2,1)} async-done(((bf16[256,6144]{1,0:T(8,128)(2,1)}), bf16[2048,6144]{1,0:T(8,128)(2,1)}) %all-gather.20.cloned.1.call-update) | async-done | bytes 25165840 | tf_op jit(solution)/shard_map/all_gather | solution.py:203
  920.8 204.4 %all-gather.22.cloned.1.call-done = bf16[6144,2048]{1,0:T(8,128)(2,1)} async-done(((bf16[768,2048]{1,0:T(8,128)(2,1)}), bf16[6144,2048]{1,0:T(8,128)(2,1)}) %all-gather.22.cloned.1.call-update) | async-done | bytes 25165840 | tf_op jit(solution)/shard_map/all_gather | solution.py:204
  1125.3 20.9 multiply_convert_fusion
  1209.6 115.0 %while.29 = (s32[]{:T(128)}, f32[1152,2,128]{0,2,1:T(8,128)}, f32[1152,2,128]{0,2,1:T(8,128)S(1)}, f32[2,576,2,2,128]{4,1,0,3,2:T(8,128)}, s32[2]{0:T(128)S(1)},...) while((s32[]{:T(128)}, f32[1152,2,128]{0,2,1:T(8,128)}, ...), condition=%wide.region_11.12_spmd.clone, body=%wide.region_9.11_spmd.clone.sunk | while | flops 3437723136 | bytes 128183776 | solution.py:270
  1228.0 16.5 fusion.192
  1244.4 17.2 fusion.190
  1285.3 16.4 fusion.192
  1301.7 17.5 fusion.190
  1451.2 18.6 convolution_convert_fusion.1
  1471.2 33.7 %convolution_convert_fusion = bf16[2048,12288]{1,0:T(8,128)(2,1)} fusion(bf16[288,2048]{1,0:T(8,128)(2,1)S(1)} %copy-done.34, bf16[288,6144]{1,0:T(8,128)(2,1)} %get-tuple-element.240, bf16[288,6144]{1,0:T(8,128)(2,1)} %get-tuple-element.241), kind=kOutput, calls=%fused_computation.61 | convolution fusion | flops 14534836224 | bytes 58589184 | tf_op jit(solution)/shard_map/dot_general | solution.py:48
  1505.2 35.3 %reduce-scatter.18.cloned.1.call-done = bf16[256,2048]{1,0:T(8,128)(2,1)} async-done(((bf16[2048,2048]{1,0:T(8,128)(2,1)}), bf16[256,2048]{1,0:T(8,128)(2,1)}) %reduce-scatter.18.cloned.1.call-update) | async-done | bytes 1048592 | tf_op jit(solution)/shard_map/reduce_scatter | solution.py:313
  1540.5 90.3 %reduce-scatter.16.cloned.1.call-done = bf16[256,2048]{1,0:T(8,128)(2,1)} async-done(((bf16[2048,2048]{1,0:T(8,128)(2,1)}), bf16[256,2048]{1,0:T(8,128)(2,1)}) %reduce-scatter.16.cloned.1.call-update) | async-done | bytes 1048592 | tf_op jit(solution)/shard_map/reduce_scatter | solution.py:310
  1630.9 90.2 %reduce-scatter.10.cloned.1.call-done = bf16[256,2048]{1,0:T(8,128)(2,1)} async-done(((bf16[2048,2048]{1,0:T(8,128)(2,1)}), bf16[256,2048]{1,0:T(8,128)(2,1)}) %reduce-scatter.10.cloned.1.call-update) | async-done | bytes 1048592 | tf_op jit(solution)/shard_map/reduce_scatter | solution.py:301
  1721.0 247.9 %reduce-scatter.20.cloned.1.call-done = bf16[768,2048]{1,0:T(8,128)(2,1)} async-done(((bf16[6144,2048]{1,0:T(8,128)(2,1)}), bf16[768,2048]{1,0:T(8,128)(2,1)}) %reduce-scatter.20.cloned.1.call-update) | async-done | bytes 3145744 | tf_op jit(solution)/shard_map/reduce_scatter | solution.py:221
  1969.0 483.8 %reduce-scatter.22.cloned.1.call-done = bf16[256,12288]{1,0:T(8,128)(2,1)} async-done(((bf16[2048,12288]{1,0:T(8,128)(2,1)}), bf16[256,12288]{1,0:T(8,128)(2,1)}) %reduce-scatter.22.cloned.1.call-update) | async-done | bytes 6291472
  2522.3 190.4 %all-reduce.8.cloned.1.call-done = (bf16[256,2048]{1,0:T(8,128)(2,1)}, bf16[256,1024]{1,0:T(8,128)(2,1)}, bf16[256,1024]{1,0:T(8,128)(2,1)}, bf16[256,2048]{1,0:...) async-done(((bf16[256,2048]{1,0:T(8,128)(2,1)}, bf16[256,1024]{1,0:T(8,128)(2,1)}, bf16[256,1024]{1,0:T(8,128)(2,1)}, ...) | async-done | bytes 13631504 | tf_op jit(solution)/shard_map/psum | solution.py:336
  (320 shorter events, 499.8 us)
Async XLA Ops:
  7.2 230.5 %all-gather.12.cloned.1.call-start = ((), (), s32[]{:S(2)}) async-start(), calls=%async_computation.18 | async-start | bytes 4718592 | tf_op jit(solution)/shard_map/all_gather | solution.py:112
  7.9 423.4 %all-gather.14.cloned.1.call-start = ((), (), s32[]{:S(2)}) async-start(), calls=%async_computation.19 | async-start | bytes 4718592 | tf_op jit(solution)/shard_map/all_gather | solution.py:113
  8.7 453.1 %all-gather.10.cloned.1.call-start = ((), (), s32[]{:S(2)}) async-start(), calls=%async_computation.17 | async-start | bytes 9437184 | tf_op jit(solution)/shard_map/all_gather | solution.py:111
  9.4 581.5 %all-gather.16.cloned.1.call-start = ((), (), s32[]{:S(2)}) async-start(), calls=%async_computation.20 | async-start | bytes 9437184 | tf_op jit(solution)/shard_map/all_gather | solution.py:115
  10.0 676.1 %all-gather.18.cloned.1.call-start = ((), (), s32[]{:S(2)}) async-start(), calls=%async_computation.21 | async-start | bytes 28311552 | tf_op jit(solution)/shard_map/all_gather | solution.py:202
  10.6 895.0 %all-gather.20.cloned.1.call-start = ((), (), s32[]{:S(2)}) async-start(), calls=%async_computation.22 | async-start | bytes 28311552 | tf_op jit(solution)/shard_map/all_gather | solution.py:203
  11.1 1114.1 %all-gather.22.cloned.1.call-start = ((), (), s32[]{:S(2)}) async-start(), calls=%async_computation.23 | async-start | bytes 28311552 | tf_op jit(solution)/shard_map/all_gather | solution.py:204
  11.9 33.3 %collective-permute-start = (bf16[256,2048]{1,0:T(8,128)(2,1)S(1)}, bf16[256,2048]{1,0:T(8,128)(2,1)S(1)}, u32[]{:S(2)}, u32[]{:S(2)}) collective-permute-start(bf16[256,2048]{1,0:T(8,128)(2,1)S(1)} %copy-done.5), channel_id=1, source_target_pairs={{0,7},{1,0},{2,1},{3,2},{4,3},{5,4},{6,5},{7,6},{8,15},{9,8},{10,9... | collective-permute-start | bytes 3145736 | tf_op jit(solution)/shard_map/ppermute | solution.py:27
  45.4 61.0 %collective-permute-start.1 = (bf16[512,2048]{1,0:T(8,128)(2,1)S(1)}, bf16[512,2048]{1,0:T(8,128)(2,1)S(1)}, u32[]{:S(2)}, u32[]{:S(2)}) collective-permute-start(bf16[512,2048]{1,0:T(8,128)(2,1)S(1)} %pad_maximum_fusion.1), channel_id=1, source_target_pairs={{0,6},{1,7},{2,0},{3,1},{4,2},{5,3},{6,4},{7,5},{8,14},{9,15},{10,... | collective-permute-start | bytes 6291464 | tf_op jit(solution)/shard_map/ppermute | solution.py:27
  108.7 315.2 %collective-permute-start.2 = (bf16[1024,2048]{1,0:T(8,128)(2,1)}, bf16[1024,2048]{1,0:T(8,128)(2,1)}, u32[]{:S(2)}, u32[]{:S(2)}) collective-permute-start(bf16[1024,2048]{1,0:T(8,128)(2,1)} %pad_maximum_fusion), channel_id=1, source_target_pairs={{0,4},{1,5},{2,6},{3,7},{4,0},{5,1},{6,2},{7,3},{8,12},{9,13},{10,... | collective-permute-start | bytes 12582920 | tf_op jit(solution)/shard_map/ppermute | solution.py:27
  242.6 200.1 %all-to-all-start.1 = ((bf16[288,8,128]{2,0,1:T(8,128)(2,1)}), bf16[288,8,128]{2,0,1:T(8,128)(2,1)}, u32[]{:S(2)}, u32[]{:S(2)}) async-start(bf16[288,8,128]{2,0,1:T(8,128)(2,1)} %bitcast.354), calls=%async_computation.1 | async-start | bytes 1179648 | tf_op jit(solution)/shard_map/all_to_all | solution.py:142
  442.7 13.5 all-to-all-start.2
  456.9 18.5 all-to-all-start.3
  475.4 19.2 all-to-all-start
  542.8 46.0 %all-to-all-start.4 = ((bf16[1152,4,128]{2,1,0:T(4,128)(2,1)}), bf16[1152,4,128]{2,1,0:T(4,128)(2,1)S(1)}, u32[]{:S(2)}, u32[]{:S(2)}) async-start(bf16[1152,4,128]{2,1,0:T(4,128)(2,1)} %copy.153), calls=%async_computation.4 | async-start | bytes 2359296 | tf_op jit(solution)/shard_map/all_to_all | solution.py:195
  1187.6 19.2 all-to-all-start.5
  1191.2 314.0 %reduce-scatter.12.cloned.1.call-start = ((), (), s32[]{:S(2)}) async-start(), calls=%async_computation.25 | async-start | bytes 4718592 | tf_op jit(solution)/shard_map/reduce_scatter | solution.py:304
  1352.5 152.8 %reduce-scatter.14.cloned.1.call-start = ((), (), s32[]{:S(2)}) async-start(), calls=%async_computation.26 | async-start | bytes 4718592 | tf_op jit(solution)/shard_map/reduce_scatter | solution.py:307
  1372.0 168.5 %reduce-scatter.18.cloned.1.call-start = ((), (), s32[]{:S(2)}) async-start(), calls=%async_computation.28 | async-start | bytes 9437184 | tf_op jit(solution)/shard_map/reduce_scatter | solution.py:313
  1381.8 249.0 %reduce-scatter.16.cloned.1.call-start = ((), (), s32[]{:S(2)}) async-start(), calls=%async_computation.27 | async-start | bytes 9437184 | tf_op jit(solution)/shard_map/reduce_scatter | solution.py:310
  1418.5 302.5 %reduce-scatter.10.cloned.1.call-start = ((), (), s32[]{:S(2)}) async-start(), calls=%async_computation.24 | async-start | bytes 9437184 | tf_op jit(solution)/shard_map/reduce_scatter | solution.py:301
  1449.9 519.0 %reduce-scatter.20.cloned.1.call-start = ((), (), s32[]{:S(2)}) async-start(), calls=%async_computation.29 | async-start | bytes 28311552 | tf_op jit(solution)/shard_map/reduce_scatter | solution.py:221
  1469.9 982.8 %reduce-scatter.22.cloned.1.call-start = ((), (), s32[]{:S(2)}) async-start(), calls=%async_computation.30 | async-start | bytes 56623104
  1504.9 1207.8 %all-reduce.8.cloned.1.call-start = ((), (), s32[]{:S(2)}) async-start(), calls=%async_computation.31 | async-start | bytes 27262976 | tf_op jit(solution)/shard_map/psum | solution.py:336
  (62 other events, 2381.3 us)
Sparse Core Ops, SparseCore 0:
  9.6 67.8 all-gather.11
  79.0 177.7 all-gather.13
  258.5 114.7 all-gather.9
  374.7 89.6 all-gather.15
  465.9 220.0 all-gather.17
  687.6 217.9 all-gather.19
  907.2 218.0 all-gather.21
  1352.6 46.4 reduce-scatter.11
  1401.9 48.3 reduce-scatter.13
  1452.5 88.0 reduce-scatter.17
  1542.8 87.9 reduce-scatter.15
  1633.0 87.9 reduce-scatter.9
  1723.4 245.5 reduce-scatter.19
  1971.2 481.4 reduce-scatter.21
  2457.3 255.2 all-reduce.7
